TPU v7x, 32 devices: a whole 2x2x4 slice. The times are simulated.
32 devices in a mesh: row: 8 (over z, core), col: 4 (over y, x).
Axes of the slice: x: 2, y: 2, z: 4, core: 2. Of those that a mesh axis runs over, the one named last changes fastest.
Arguments:
- sire_index: int32 [1024], P('row'), may hold values from 0 to 4095
- dam_index: int32 [1024], P('row'), may hold values from -1 to 4095, as said below
- relatives: float32 [4096, 4, 2048], P('row', None, 'col'), may hold values from 0 to 1
- factor_blocks: float32 [6, 2048, 2048], P(None, 'row', 'col'), may hold values from -0.125 to 0.125
- inverses: float32 [4, 2048, 2048], P(None, 'col'), as said below
Outputs:
- relationship: float32 [4, 2048, 1024], P(None, 'col', 'row')
- border: float32 [4, 2048, 1024], P(None, 'col', 'row')
Inputs may be any that keep to these rules, and one draw needn't show every extreme that they name: `dam_index`: -1 marks an unknown dam; every other value is a row of relatives. `inverses`: lower triangular, with diagonal entries of 0.6 to 1.4.
All inputs are finite; a program needn't handle non-finite values.
Results may differ from a plain program's by a relative error of at most 0.0001.
Values sent between devices are 32-bit elements; how exact they have to be, the bound alone decides.
A program may use at most 128 MiB of HBM per device.

v0:
```python
import jax
import jax.numpy as jnp
from jax import lax
from jax.sharding import PartitionSpec as P


def product(left, right):
    return jnp.dot(left, right, precision=lax.Precision.HIGHEST, preferred_element_type=jnp.float32)


def fetch_rows(stacked):
    return lax.all_gather(stacked, "row", axis=0, tiled=True)


def per_device(sire_index, dam_index, relatives, factor_blocks, inverses):
    calf_dev = sire_index.shape[0]
    old_dev, blocks, block_cols = relatives.shape
    flat_rows = relatives.reshape(old_dev, blocks * block_cols)
    all_sires, all_dams = (
        lax.all_gather(sire_index, "row", axis=0, tiled=True),
        lax.all_gather(dam_index, "row", axis=0, tiled=True),
    )
    owned = lax.axis_index("row") * old_dev + lax.iota(jnp.int32, old_dev)
    picks = 0.5 * (
        (all_sires[:, None] == owned[None, :]).astype(jnp.float32)
        + (all_dams[:, None] == owned[None, :]).astype(jnp.float32)
    )
    mine = lax.psum_scatter(product(picks, flat_rows), "row", scatter_dimension=0, tiled=True)
    relation = mine.T
    relationship = relation.reshape(blocks, block_cols, calf_dev)
    solved = []
    for target in range(blocks):
        remain = relationship[target]
        if target > 0:
            needed = jnp.stack(
                [factor_blocks[target * (target - 1) // 2 + source] for source in range(target)],
                axis=1,
            )
            whole_rows = fetch_rows(needed).reshape(-1, target * block_cols)
            earlier = jnp.concatenate(solved, axis=0)

            def earlier_terms(start, count, whole_rows=whole_rows, earlier=earlier):
                return product(whole_rows, earlier)

            remain = remain - lax.psum_scatter(
                earlier_terms(jnp.int32(0), block_cols * lax.axis_size("col")),
                "col",
                scatter_dimension=0,
                tiled=True,
            )
        own_inverse = inverses[target]
        solved.append(product(own_inverse, lax.all_gather(remain, "col", axis=0, tiled=True)))
    return (relationship, jnp.stack(solved))


def solution(mesh):
    return jax.shard_map(
        per_device,
        mesh=mesh,
        in_specs=(
            P("row"),
            P("row"),
            P("row", None, "col"),
            P(None, "row", "col"),
            P(None, "col", None),
        ),
        out_specs=(P(None, "col", "row"), P(None, "col", "row")),
        check_vma=False,
    )
```

profile of v0, /device:TPU:0, one launch (start us, length us, event | category | flops | bytes accessed | tf_op | source)
XLA Modules:
  0.0 627.8 jit_solution(4835952748387480247)
XLA Ops:
  7.2 0.0 reduce-scatter.5.cloned.1.call-start
  7.2 6.1 copy.33
  13.4 13.4 %all-gather.1 = s32[8,1,128]{2,1,0:T(1,128)S(1)} all-gather(s32[1,1,128]{2,1,0:T(1,128)S(1)} %bitcast.82), channel_id=1, replica_groups=mesh['row'=8,'col'=4] {'row'}, dimensions={0}, use_global_device_ids=true | all-gather | bytes 4608 | tf_op jit(solution)/shard_map/all_gather | solution.py:20
  26.8 8.7 %all-gather.2 = s32[8,1,128]{2,1,0:T(1,128)S(1)} all-gather(s32[1,1,128]{2,1,0:T(1,128)S(1)} %bitcast.83), channel_id=1, replica_groups=mesh['row'=8,'col'=4] {'row'}, dimensions={0}, use_global_device_ids=true | all-gather | bytes 4608 | tf_op jit(solution)/shard_map/all_gather | solution.py:21
  35.5 17.8 %fusion.17 = f32[1024,2048]{1,0:T(8,128)} fusion(f32[512,2048]{1,0:T(8,128)} %bitcast.68, s32[512]{0:T(512)S(1)} %iota_add_fusion, s32[1024]{0:T(1024)S(1)} %bitcast.81, s32[1024]{0:T(1024)S(1)} %bitcast.80), kind=kOutput, calls=%fused_computation.15 | convolution fusion | flops 12888047616 | bytes 12593152 | tf_op jit(solution)/shard_map/dot_general | solution.py:8
  53.4 0.0 all-gather.11.cloned.1.call-start
  53.5 89.0 %reduce-scatter.5.cloned.1.call-done = f32[128,2048]{1,0:T(8,128)} async-done(((f32[1024,2048]{1,0:T(8,128)}), f32[128,2048]{1,0:T(8,128)}) %reduce-scatter.5.cloned.1.call-update) | async-done | bytes 1048592 | tf_op jit(solution)/shard_map/reduce_scatter | solution.py:28
  142.4 1.7 slice.60
  144.1 0.0 all-gather.23.cloned.1.call-start
  144.2 3.2 fusion.44
  147.4 0.2 reduce-scatter.7.cloned.1.call-start
  147.6 21.7 %all-gather.11.cloned.1.call-done = f32[2048,128]{0,1:T(8,128)} async-done(((f32[512,128]{0,1:T(8,128)}), f32[2048,128]{0,1:T(8,128)}) %all-gather.11.cloned.1.call-update) | async-done | bytes 1048592 | tf_op jit(solution)/shard_map/all_gather | solution.py:52
  169.3 6.9 %fusion.8 = f32[128,512]{1,0:T(8,128)S(1)} fusion(f32[2048,128]{0,1:T(8,128)} %all-gather.11.cloned.1.call-done, f32[4,512,2048]{2,1,0:T(8,128)} %param.9), kind=kOutput, calls=%fused_computation.8 | convolution fusion | flops 1610612736 | bytes 5505024 | tf_op jit(solution)/shard_map/dot_general | solution.py:8
  176.1 42.2 %all-gather.23.cloned.1.call-done = f32[1,2048,512]{2,1,0:T(8,128)} async-done(((f32[1,256,512]{2,1,0:T(8,128)}), f32[1,2048,512]{2,1,0:T(8,128)}) %all-gather.23.cloned.1.call-update) | async-done | bytes 4194320 | tf_op jit(solution)/shard_map/all_gather | solution.py:12
  218.3 7.5 %fusion.14 = f32[2048,128]{0,1:T(8,128)} fusion(f32[128,512]{1,0:T(8,128)S(1)} %fusion.8, f32[1,2048,512]{2,1,0:T(8,128)} %all-gather.23.cloned.1.call-done), kind=kOutput, calls=%fused_computation.14 | convolution fusion | flops 1610612736 | bytes 5505024 | tf_op jit(solution)/shard_map/dot_general | solution.py:8
  225.8 0.0 all-gather.13.cloned.1.call-start
  225.9 26.8 %reduce-scatter.7.cloned.1.call-done = f32[512,128]{0,1:T(8,128)} async-done(((f32[2048,128]{0,1:T(8,128)}), f32[512,128]{0,1:T(8,128)}) %reduce-scatter.7.cloned.1.call-update) | async-done | bytes 262160 | tf_op jit(solution)/shard_map/reduce_scatter | solution.py:45
  252.7 1.7 slice_subtract_fusion.2
  254.4 0.0 all-gather.15.cloned.1.call-start
  254.5 2.1 copy.28
  256.5 2.0 copy.29
  258.6 2.2 pad_maximum_fusion.1
  260.8 0.3 reduce-scatter.9.cloned.1.call-start
  261.1 20.0 %all-gather.13.cloned.1.call-done = f32[2048,128]{0,1:T(8,128)} async-done(((f32[512,128]{0,1:T(8,128)}), f32[2048,128]{0,1:T(8,128)}) %all-gather.13.cloned.1.call-update) | async-done | bytes 1048592 | tf_op jit(solution)/shard_map/all_gather | solution.py:52
  281.1 6.9 %fusion.4 = f32[128,512]{1,0:T(8,128)S(1)} fusion(f32[2048,128]{0,1:T(8,128)} %all-gather.13.cloned.1.call-done, f32[4,512,2048]{2,1,0:T(8,128)} %param.9), kind=kOutput, calls=%fused_computation.4 | convolution fusion | flops 1610612736 | bytes 5505024 | tf_op jit(solution)/shard_map/dot_general | solution.py:8
  287.9 77.2 %all-gather.15.cloned.1.call-done = f32[2048,2,512]{0,2,1:T(8,128)} async-done(((f32[256,2,512]{0,2,1:T(8,128)}), f32[2048,2,512]{0,2,1:T(8,128)}) %all-gather.15.cloned.1.call-update) | async-done | bytes 8388624 | tf_op jit(solution)/shard_map/all_gather | solution.py:12
  365.2 8.1 %fusion.37 = f32[2048,128]{0,1:T(8,128)} fusion(f32[2048,1024]{0,1:T(8,128)} %bitcast.58, f32[512,128]{0,1:T(8,128)S(1)} %bitcast.69, f32[512,128]{0,1:T(8,128)S(1)} %bitcast.59), kind=kOutput, calls=%fused_computation.36 | convolution fusion | flops 3221356544 | bytes 9961472 | tf_op jit(solution)/shard_map/dot_general | solution.py:8
  373.3 0.0 all-gather.17.cloned.1.call-start
  373.3 26.5 %reduce-scatter.9.cloned.1.call-done = f32[512,128]{0,1:T(8,128)} async-done(((f32[2048,128]{0,1:T(8,128)}), f32[512,128]{0,1:T(8,128)}) %reduce-scatter.9.cloned.1.call-update) | async-done | bytes 262160 | tf_op jit(solution)/shard_map/reduce_scatter | solution.py:45
  399.8 1.7 slice_subtract_fusion.1
  401.6 0.0 all-gather.19.cloned.1.call-start
  401.6 1.0 copy.30
  402.6 0.2 copy.31
  402.8 0.2 copy.32
  403.0 2.3 pad_maximum_fusion
  405.4 0.3 reduce-scatter.11.cloned.1.call-start
  405.7 23.1 %all-gather.17.cloned.1.call-done = f32[2048,128]{0,1:T(8,128)} async-done(((f32[512,128]{0,1:T(8,128)}), f32[2048,128]{0,1:T(8,128)}) %all-gather.17.cloned.1.call-update) | async-done | bytes 1048592 | tf_op jit(solution)/shard_map/all_gather | solution.py:52
  428.8 6.9 %fusion.2 = f32[128,512]{1,0:T(8,128)S(1)} fusion(f32[2048,128]{0,1:T(8,128)} %all-gather.17.cloned.1.call-done, f32[4,512,2048]{2,1,0:T(8,128)} %param.9), kind=kOutput, calls=%fused_computation.2 | convolution fusion | flops 1610612736 | bytes 5505024 | tf_op jit(solution)/shard_map/dot_general | solution.py:8
  435.7 111.5 %all-gather.19.cloned.1.call-done = f32[2048,3,512]{0,2,1:T(8,128)} async-done(((f32[256,3,512]{0,2,1:T(8,128)}), f32[2048,3,512]{0,2,1:T(8,128)}) %all-gather.19.cloned.1.call-update) | async-done | bytes 12582928 | tf_op jit(solution)/shard_map/all_gather | solution.py:12
  547.2 10.6 %fusion.31 = f32[2048,128]{0,1:T(8,128)} fusion(f32[2048,1536]{0,1:T(8,128)} %bitcast.57, f32[512,128]{0,1:T(8,128)S(1)} %bitcast.72, f32[512,128]{0,1:T(8,128)S(1)} %bitcast.70, f32[512,128]{0,1:T(8,128)S(1)} %bitcast.60), kind=kOutput, calls=%fused_computation.30 | convolution fusion | flops 4832231424 | bytes 14417920 | tf_op jit(solution)/shard_map/dot_general | solution.py:8
  557.8 0.0 all-gather.21.cloned.1.call-start
  557.9 26.2 %reduce-scatter.11.cloned.1.call-done = f32[512,128]{0,1:T(8,128)} async-done(((f32[2048,128]{0,1:T(8,128)}), f32[512,128]{0,1:T(8,128)}) %reduce-scatter.11.cloned.1.call-update) | async-done | bytes 262160 | tf_op jit(solution)/shard_map/reduce_scatter | solution.py:45
  584.1 1.7 slice_subtract_fusion
  585.8 1.3 copy.27
  587.1 26.0 %all-gather.21.cloned.1.call-done = f32[2048,128]{0,1:T(8,128)} async-done(((f32[512,128]{0,1:T(8,128)}), f32[2048,128]{0,1:T(8,128)}) %all-gather.21.cloned.1.call-update) | async-done | bytes 1048592 | tf_op jit(solution)/shard_map/all_gather | solution.py:52
  613.0 6.9 %fusion.24 = f32[1,512,128]{1,2,0:T(8,128)S(1)} fusion(f32[2048,128]{0,1:T(8,128)} %all-gather.21.cloned.1.call-done, f32[4,512,2048]{2,1,0:T(8,128)} %param.9), kind=kOutput, calls=%fused_computation.23 | convolution fusion | flops 1610612736 | bytes 5505024 | tf_op jit(solution)/shard_map/dot_general | solution.py:8
  619.9 0.1 pad_maximum_fusion.2
  620.0 1.3 copy.24
  (18 shorter events, 0.2 us)
Async XLA Ops:
  7.2 135.3 %reduce-scatter.5.cloned.1.call-start = ((), (), s32[]{:S(2)}) async-start(), calls=%async_computation.4 | async-start | bytes 9437184 | tf_op jit(solution)/shard_map/reduce_scatter | solution.py:28
  7.2 6.2 copy-start.1
  7.2 19.6 %copy-start.2 = (s32[128]{0:T(128)S(1)}, s32[128]{0:T(128)}, u32[]{:S(2)}) copy-start(s32[128]{0:T(128)} %param.6) | copy-start | bytes 1540
  53.4 115.8 %all-gather.11.cloned.1.call-start = ((), (), s32[]{:S(2)}) async-start(), calls=%async_computation.5 | async-start | bytes 1310720 | tf_op jit(solution)/shard_map/all_gather | solution.py:52
  144.1 74.2 %all-gather.23.cloned.1.call-start = ((), (), s32[]{:S(2)}) async-start(), calls=%async_computation.14 | async-start | bytes 4718592 | tf_op jit(solution)/shard_map/all_gather | solution.py:12
  147.4 105.3 %reduce-scatter.7.cloned.1.call-start = ((), (), s32[]{:S(2)}) async-start(), calls=%async_computation.6 | async-start | bytes 1310720 | tf_op jit(solution)/shard_map/reduce_scatter | solution.py:45
  176.1 76.6 %copy-start = (f32[128,2048]{1,0:T(8,128)S(1)}, f32[128,2048]{1,0:T(8,128)}, u32[]{:S(2)}) copy-start(f32[128,2048]{1,0:T(8,128)} %reduce-scatter.5.cloned.1.call-done) | copy-start | bytes 3145732
  225.8 55.3 %all-gather.13.cloned.1.call-start = ((), (), s32[]{:S(2)}) async-start(), calls=%async_computation.7 | async-start | bytes 1310720 | tf_op jit(solution)/shard_map/all_gather | solution.py:52
  254.4 110.8 %all-gather.15.cloned.1.call-start = ((), (), s32[]{:S(2)}) async-start(), calls=%async_computation.8 | async-start | bytes 9437184 | tf_op jit(solution)/shard_map/all_gather | solution.py:12
  260.8 139.0 %reduce-scatter.9.cloned.1.call-start = ((), (), s32[]{:S(2)}) async-start(), calls=%async_computation.9 | async-start | bytes 1310720 | tf_op jit(solution)/shard_map/reduce_scatter | solution.py:45
  373.3 55.5 %all-gather.17.cloned.1.call-start = ((), (), s32[]{:S(2)}) async-start(), calls=%async_computation.10 | async-start | bytes 1310720 | tf_op jit(solution)/shard_map/all_gather | solution.py:52
  401.6 145.6 %all-gather.19.cloned.1.call-start = ((), (), s32[]{:S(2)}) async-start(), calls=%async_computation.11 | async-start | bytes 14155776 | tf_op jit(solution)/shard_map/all_gather | solution.py:12
  405.4 178.7 %reduce-scatter.11.cloned.1.call-start = ((), (), s32[]{:S(2)}) async-start(), calls=%async_computation.12 | async-start | bytes 1310720 | tf_op jit(solution)/shard_map/reduce_scatter | solution.py:45
  557.8 55.2 %all-gather.21.cloned.1.call-start = ((), (), s32[]{:S(2)}) async-start(), calls=%async_computation.13 | async-start | bytes 1310720 | tf_op jit(solution)/shard_map/all_gather | solution.py:52
Sparse Core Ops, SparseCore 0:
  53.5 88.8 reduce-scatter.4
  144.3 24.9 all-gather.10
  171.4 46.8 all-gather.22
  225.9 26.7 reduce-scatter.6
  254.5 26.4 all-gather.12
  283.1 82.0 all-gather.14
  373.4 26.4 reduce-scatter.8
  402.3 26.4 all-gather.16
  430.4 116.6 all-gather.18
  557.9 26.0 reduce-scatter.10
  586.5 26.4 all-gather.20
where the time goes:
time: 628 us
  waiting for transfers between devices  490 us (78%)
  matrix products  71.4 us (11%)
  blocking collectives  22.2 us (4%)
  local copies, waits for them, and re-layouts  19.1 us (3%)
  between operations  14 us (2%)
  other arithmetic  9.71 us (2%)
    all_gather x3, waiting for transfers between devices, fetch_rows(): return lax.all_gather(stacked, 'row', axis=0, tiled=True)  231 us
    all_gather x4, waiting for transfers between devices, per_device(): lax.all_gather(remain, 'col', axis=0, tiled=True)  90.7 us
    reduce_scatter x1, waiting for transfers between devices, per_device(): lax.psum_scatter(product(picks, flat_rows), 'row', scatter_dimension=0, t...  89 us
    reduce_scatter x3, waiting for transfers between devices, per_device(): lax.psum_scatter(earlier_terms(jnp.int32(0), block_cols * lax.axis_size('...  79.6 us
    dot_general x8, matrix products, product(): jnp.dot(left, right, precision=lax.Precision.HIGHEST, preferred_element_t...  71.4 us
    unnamed x14, local copies, waits for them, and re-layouts  14.2 us
    all_gather x1, blocking collectives, per_device(): lax.all_gather(sire_index, 'row', axis=0, tiled=True)  13.4 us
  transfers between devices with their start and end apart: 11, of which 11 were waited for; matrix products, arithmetic and copies ran while one was open for 6% of the time, Pallas kernels for 0%

commit v1 on v0

--- a/solution.py
+++ b/solution.py
@@ -2,6 +2,19 @@
 import jax.numpy as jnp
 from jax import lax
 from jax.sharding import PartitionSpec as P
+
+
+def collect(value, axis, dim):
+    peers, place, rows = (lax.axis_size(axis), lax.axis_index(axis), value.shape[dim])
+    upward = [(i, (i + 1) % peers) for i in range(peers)]
+    whole = jnp.zeros((*value.shape[:dim], peers * rows, *value.shape[dim + 1 :]), value.dtype)
+    current = value
+    for step in range(peers):
+        owner = (place - step) % peers
+        whole = lax.dynamic_update_slice_in_dim(whole, current, owner * rows, axis=dim)
+        if step < peers - 1:
+            current = lax.ppermute(current, axis, upward)
+    return whole
 
 
 def product(left, right):
@@ -9,7 +22,7 @@
 
 
 def fetch_rows(stacked):
-    return lax.all_gather(stacked, "row", axis=0, tiled=True)
+    return collect(stacked, "row", 0)
 
 
 def per_device(sire_index, dam_index, relatives, factor_blocks, inverses):

time: 628 us -> 507 us (0.81); the launches traced: 628 us -> 498 us
  waiting for transfers between devices: 490 us -> 298 us
  local copies, waits for them, and re-layouts: 19.1 us -> 80.9 us
    ppermute x0 -> x21, waiting for transfers between devices: none -> 233 us  [collect(): current = lax.ppermute(current, axis, upward)]
    all_gather x3 -> x0, waiting for transfers between devices: 231 us -> none  [fetch_rows(): return lax.all_gather(stacked, 'row', axis=0, tiled=True)]
    reduce_scatter x1, waiting for transfers between devices: 89 us -> 0.01 us  [per_device(): lax.psum_scatter(product(picks, flat_rows), 'row', scatter_dimension=0, t...]
    all_gather x4, waiting for transfers between devices: 90.7 us -> 33.5 us  [per_device(): lax.all_gather(remain, 'col', axis=0, tiled=True)]
    reduce_scatter x3, waiting for transfers between devices: 79.6 us -> 31.5 us  [per_device(): lax.psum_scatter(earlier_terms(jnp.int32(0), block_cols * lax.axis_size('...]
    dynamic_update_slice x0 -> x22, local copies, waits for them, and re-layouts: none -> 44.8 us  [collect(): lax.dynamic_update_slice_in_dim(whole, current, owner * rows, axis=dim)]
    broadcast_in_dim x0 -> x2, local copies, waits for them, and re-layouts: none -> 10.5 us  [collect(): jnp.zeros((*value.shape[:dim], peers * rows, *value.shape[dim + 1:]), val...]
    unnamed x14 -> x28, local copies, waits for them, and re-layouts: 14.2 us -> 19.7 us
  transfers between devices with their start and end apart: 11 -> 29, of which waited for: 11 -> 18; matrix products, arithmetic and copies ran while one was open for 6% -> 22% of each run, Pallas kernels for 0% -> 0%
where the time goes in v1:
time: 507 us; the launch traced here: 498 us
  waiting for transfers between devices  298 us (59%)
  local copies, waits for them, and re-layouts  80.9 us (16%)
  matrix products  70.1 us (14%)
  blocking collectives  22.2 us (4%)
  between operations  14.6 us (3%)
  other arithmetic  8.38 us (2%)
    ppermute x21, waiting for transfers between devices, collect(): current = lax.ppermute(current, axis, upward)  233 us
    dot_general x8, matrix products, product(): jnp.dot(left, right, precision=lax.Precision.HIGHEST, preferred_element_t...  70.1 us
    dynamic_update_slice x22, local copies, waits for them, and re-layouts, collect(): lax.dynamic_update_slice_in_dim(whole, current, owner * rows, axis=dim)  44.8 us
    all_gather x4, waiting for transfers between devices, per_device(): lax.all_gather(remain, 'col', axis=0, tiled=True)  33.5 us
    reduce_scatter x3, waiting for transfers between devices, per_device(): lax.psum_scatter(earlier_terms(jnp.int32(0), block_cols * lax.axis_size('...  31.5 us
    unnamed x28, local copies, waits for them, and re-layouts  19.7 us
    all_gather x1, blocking collectives, per_device(): lax.all_gather(sire_index, 'row', axis=0, tiled=True)  13.5 us
    broadcast_in_dim x2, local copies, waits for them, and re-layouts, collect(): jnp.zeros((*value.shape[:dim], peers * rows, *value.shape[dim + 1:]), val...  10.5 us
  transfers between devices with their start and end apart: 29, of which 18 were waited for; matrix products, arithmetic and copies ran while one was open for 22% of the time, Pallas kernels for 0%

profile of v1, /device:TPU:0, one launch (start us, length us, event | category | flops | bytes accessed | tf_op | source)
XLA Modules:
  0.0 497.7 jit_solution(8394106655780898703)
XLA Ops:
  7.2 4.2 copy.35
  11.4 13.5 %all-gather = s32[8,1,128]{2,1,0:T(1,128)S(1)} all-gather(s32[1,1,128]{2,1,0:T(1,128)S(1)} %bitcast.92), channel_id=1, replica_groups=mesh['row'=8,'col'=4] {'row'}, dimensions={0}, use_global_device_ids=true | all-gather | bytes 4608 | tf_op jit(solution)/shard_map/all_gather | solution.py:33
  24.9 8.7 %all-gather.1 = s32[8,1,128]{2,1,0:T(1,128)S(1)} all-gather(s32[1,1,128]{2,1,0:T(1,128)S(1)} %bitcast.93), channel_id=1, replica_groups=mesh['row'=8,'col'=4] {'row'}, dimensions={0}, use_global_device_ids=true | all-gather | bytes 4608 | tf_op jit(solution)/shard_map/all_gather | solution.py:34
  33.6 16.3 %fusion.12 = f32[1024,2048]{1,0:T(8,128)} fusion(f32[512,2048]{1,0:T(8,128)S(1)} %bitcast.78, s32[512]{0:T(512)S(1)} %iota_add_fusion, s32[1024]{0:T(1024)S(1)} %bitcast.91, s32[1024]{0:T(1024)S(1)} %bitcast.90), kind=kOutput, calls=%fused_computation.12 | convolution fusion | flops 12888047616 | bytes 12593152 | tf_op jit(solution)/shard_map/dot_general | solution.py:21
  53.8 2.0 copy.30
  55.9 2.1 copy.31
  57.9 4.4 broadcast_in_dim.4
  65.0 8.8 %collective-permute-done = f32[256,1,512]{2,0,1:T(8,128)} collective-permute-done((f32[256,1,512]{2,0,1:T(8,128)}, f32[256,1,512]{2,0,1:T(8,128)}, u32[]{:S(2)}, u32[]{:S(2)}) %collective-permute-start) | collective-permute-done | bytes 524320 | tf_op jit(solution)/shard_map/ppermute | solution.py:16
  73.9 50.5 %collective-permute-done.1 = f32[256,1,512]{2,0,1:T(8,128)S(1)} collective-permute-done((f32[256,1,512]{2,0,1:T(8,128)}, f32[256,1,512]{2,0,1:T(8,128)S(1)}, u32[]{:S(2)}, u32[]{:S(2)}) %collective-permute-start.1) | collective-permute-done | bytes 524320 | tf_op jit(solution)/shard_map/ppermute | solution.py:16
  125.7 20.5 %collective-permute-done.2 = f32[256,1,512]{2,0,1:T(8,128)} collective-permute-done((f32[256,1,512]{2,0,1:T(8,128)S(1)}, f32[256,1,512]{2,0,1:T(8,128)}, u32[]{:S(2)}, u32[]{:S(2)}) %collective-permute-start.2) | collective-permute-done | bytes 524320 | tf_op jit(solution)/shard_map/ppermute | solution.py:16
  146.7 2.1 copy.32
  148.7 2.0 copy.33
  150.8 2.1 copy.34
  152.8 6.1 %broadcast_in_dim.5 = f32[2048,3,512]{0,2,1:T(8,128)} broadcast(f32[]{:T(128)} %constant.108.clone.1), dimensions={} | broadcast | bytes 12582916 | tf_op jit(solution)/shard_map/broadcast_in_dim | solution.py:10
  159.0 2.0 pad_maximum_fusion
  161.0 21.2 %collective-permute-done.3 = f32[256,1,512]{2,0,1:T(8,128)} collective-permute-done((f32[256,1,512]{2,0,1:T(8,128)}, f32[256,1,512]{2,0,1:T(8,128)}, u32[]{:S(2)}, u32[]{:S(2)}) %collective-permute-start.3) | collective-permute-done | bytes 524320 | tf_op jit(solution)/shard_map/ppermute | solution.py:16
  182.2 2.5 reshape.68
  185.5 19.1 %collective-permute-done.4 = f32[256,1,512]{2,0,1:T(8,128)} collective-permute-done((f32[256,1,512]{2,0,1:T(8,128)}, f32[256,1,512]{2,0,1:T(8,128)}, u32[]{:S(2)}, u32[]{:S(2)}) %collective-permute-start.4) | collective-permute-done | bytes 524320 | tf_op jit(solution)/shard_map/ppermute | solution.py:16
  212.1 9.3 %collective-permute-done.5 = f32[256,1,512]{2,0,1:T(8,128)S(1)} collective-permute-done((f32[256,1,512]{2,0,1:T(8,128)}, f32[256,1,512]{2,0,1:T(8,128)S(1)}, u32[]{:S(2)}, u32[]{:S(2)}) %collective-permute-start.5) | collective-permute-done | bytes 524320 | tf_op jit(solution)/shard_map/ppermute | solution.py:16
  226.0 17.9 %collective-permute-done.6 = f32[256,1,512]{2,0,1:T(8,128)S(1)} collective-permute-done((f32[256,1,512]{2,0,1:T(8,128)S(1)}, f32[256,1,512]{2,0,1:T(8,128)S(1)}, u32[]{:S(2)}, u32[]{:S(2)}) %collective-permute-start.6) | collective-permute-done | bytes 524320 | tf_op jit(solution)/shard_map/ppermute | solution.py:16
  244.7 6.9 %fusion.6 = f32[128,512]{1,0:T(8,128)S(1)} fusion(f32[2048,128]{0,1:T(8,128)} %all-gather.7.cloned.1.call-done, f32[4,512,2048]{2,1,0:T(8,128)} %param.9), kind=kOutput, calls=%fused_computation.6 | convolution fusion | flops 1610612736 | bytes 5505024 | tf_op jit(solution)/shard_map/dot_general | solution.py:21
  251.6 7.7 %fusion.39 = f32[2048,128]{0,1:T(8,128)} fusion(f32[2048,512]{1,0:T(8,128)} %bitcast_dynamic-update-slice_fusion, f32[128,512]{1,0:T(8,128)S(1)} %fusion.6), kind=kOutput, calls=%fused_computation.69 | convolution fusion | flops 1610612736 | bytes 5505024 | tf_op jit(solution)/shard_map/dot_general | solution.py:21
  259.5 32.9 %collective-permute-done.11 = f32[256,2,512]{0,2,1:T(8,128)} collective-permute-done((f32[256,2,512]{0,2,1:T(8,128)}, f32[256,2,512]{0,2,1:T(8,128)}, u32[]{:S(2)}, u32[]{:S(2)}) %collective-permute-start.11) | collective-permute-done | bytes 1048608 | tf_op jit(solution)/shard_map/ppermute | solution.py:16
  294.2 14.5 %collective-permute-done.12 = f32[256,2,512]{0,2,1:T(8,128)} collective-permute-done((f32[256,2,512]{0,2,1:T(8,128)}, f32[256,2,512]{0,2,1:T(8,128)}, u32[]{:S(2)}, u32[]{:S(2)}) %collective-permute-start.12) | collective-permute-done | bytes 1048608 | tf_op jit(solution)/shard_map/ppermute | solution.py:16
  308.7 2.3 constant_dynamic-update-slice_fusion.14
  311.0 2.3 constant_dynamic-update-slice_fusion.13
  313.4 2.4 constant_dynamic-update-slice_fusion.12
  315.7 2.3 constant_dynamic-update-slice_fusion.11
  318.0 2.3 constant_dynamic-update-slice_fusion.10
  320.4 5.2 %collective-permute-done.17 = f32[256,3,512]{0,2,1:T(8,128)} collective-permute-done((f32[256,3,512]{0,2,1:T(8,128)}, f32[256,3,512]{0,2,1:T(8,128)}, u32[]{:S(2)}, u32[]{:S(2)}) %collective-permute-start.17) | collective-permute-done | bytes 1572896 | tf_op jit(solution)/shard_map/ppermute | solution.py:16
  325.7 2.4 constant_dynamic-update-slice_fusion.9
  328.1 8.6 %collective-permute-done.13 = f32[256,2,512]{0,2,1:T(8,128)S(1)} collective-permute-done((f32[256,2,512]{0,2,1:T(8,128)}, f32[256,2,512]{0,2,1:T(8,128)S(1)}, u32[]{:S(2)}, u32[]{:S(2)}) %collective-permute-start.13) | collective-permute-done | bytes 1048608 | tf_op jit(solution)/shard_map/ppermute | solution.py:16
  337.8 6.9 %fusion.4 = f32[128,512]{1,0:T(8,128)S(1)} fusion(f32[2048,128]{0,1:T(8,128)} %all-gather.9.cloned.1.call-done, f32[4,512,2048]{2,1,0:T(8,128)} %param.9), kind=kOutput, calls=%fused_computation.4 | convolution fusion | flops 1610612736 | bytes 5505024 | tf_op jit(solution)/shard_map/dot_general | solution.py:21
  344.7 8.1 %fusion.32 = f32[2048,128]{0,1:T(8,128)} fusion(f32[2048,1024]{0,1:T(8,128)} %bitcast.23, f32[512,128]{0,1:T(8,128)S(1)} %bitcast.79, f32[512,128]{0,1:T(8,128)S(1)} %bitcast.69), kind=kOutput, calls=%fused_computation.33 | convolution fusion | flops 3221356544 | bytes 9961472 | tf_op jit(solution)/shard_map/dot_general | solution.py:21
  353.6 22.0 %collective-permute-done.19 = f32[256,3,512]{0,2,1:T(8,128)} collective-permute-done((f32[256,3,512]{0,2,1:T(8,128)}, f32[256,3,512]{0,2,1:T(8,128)}, u32[]{:S(2)}, u32[]{:S(2)}) %collective-permute-start.19) | collective-permute-done | bytes 1572896 | tf_op jit(solution)/shard_map/ppermute | solution.py:16
  375.6 3.5 reduce-scatter.9.cloned.1.call-done
  381.1 2.7 constant_dynamic-update-slice_fusion.6
  385.1 2.7 constant_dynamic-update-slice_fusion.4
  387.8 2.8 constant_dynamic-update-slice_fusion.3
  390.6 2.7 constant_dynamic-update-slice_fusion.2
  393.3 2.7 constant_dynamic-update-slice_fusion.1
  397.5 2.7 constant_dynamic-update-slice_fusion
  400.3 7.6 %all-gather.11.cloned.1.call-done = f32[2048,128]{0,1:T(8,128)} async-done(((f32[512,128]{0,1:T(8,128)}), f32[2048,128]{0,1:T(8,128)}) %all-gather.11.cloned.1.call-update) | async-done | bytes 1048592 | tf_op jit(solution)/shard_map/all_gather | solution.py:65
  407.9 6.9 %fusion.2 = f32[128,512]{1,0:T(8,128)S(1)} fusion(f32[2048,128]{0,1:T(8,128)} %all-gather.11.cloned.1.call-done, f32[4,512,2048]{2,1,0:T(8,128)} %param.9), kind=kOutput, calls=%fused_computation.2 | convolution fusion | flops 1610612736 | bytes 5505024 | tf_op jit(solution)/shard_map/dot_general | solution.py:21
  414.7 10.6 %fusion.26 = f32[2048,128]{0,1:T(8,128)} fusion(f32[2048,1536]{0,1:T(8,128)} %bitcast.30, f32[512,128]{0,1:T(8,128)S(1)} %bitcast.82, f32[512,128]{0,1:T(8,128)S(1)} %bitcast.80, f32[512,128]{0,1:T(8,128)S(1)} %bitcast.70), kind=kOutput, calls=%fused_computation.27 | convolution fusion | flops 4832231424 | bytes 14417920 | tf_op jit(solution)/shard_map/dot_general | solution.py:21
  425.4 28.0 %reduce-scatter.11.cloned.1.call-done = f32[512,128]{0,1:T(8,128)} async-done(((f32[2048,128]{0,1:T(8,128)}), f32[512,128]{0,1:T(8,128)}) %reduce-scatter.11.cloned.1.call-update) | async-done | bytes 262160 | tf_op jit(solution)/shard_map/reduce_scatter | solution.py:58
  456.5 25.9 %all-gather.13.cloned.1.call-done = f32[2048,128]{0,1:T(8,128)} async-done(((f32[512,128]{0,1:T(8,128)}), f32[2048,128]{0,1:T(8,128)}) %all-gather.13.cloned.1.call-update) | async-done | bytes 1048592 | tf_op jit(solution)/shard_map/all_gather | solution.py:65
  482.4 6.9 %fusion.19 = f32[1,512,128]{1,2,0:T(8,128)S(1)} fusion(f32[2048,128]{0,1:T(8,128)} %all-gather.13.cloned.1.call-done, f32[4,512,2048]{2,1,0:T(8,128)} %param.9), kind=kOutput, calls=%fused_computation.20 | convolution fusion | flops 1610612736 | bytes 5505024 | tf_op jit(solution)/shard_map/dot_general | solution.py:21
  (90 shorter events, 35.7 us)
Async XLA Ops:
  7.2 197.5 %reduce-scatter.5.cloned.1.call-start = ((), (), s32[]{:S(2)}) async-start(), calls=%async_computation.4 | async-start | bytes 9437184 | tf_op jit(solution)/shard_map/reduce_scatter | solution.py:41
  7.2 4.2 copy-start.8
  7.2 17.6 %copy-start.9 = (s32[128]{0:T(128)S(1)}, s32[128]{0:T(128)}, u32[]{:S(2)}) copy-start(s32[128]{0:T(128)} %param.6) | copy-start | bytes 1540
  49.9 1.9 copy-start
  49.9 194.8 %all-gather.7.cloned.1.call-start = ((), (), s32[]{:S(2)}) async-start(), calls=%async_computation.5 | async-start | bytes 1310720 | tf_op jit(solution)/shard_map/all_gather | solution.py:65
  53.5 20.4 %collective-permute-start = (f32[256,1,512]{2,0,1:T(8,128)}, f32[256,1,512]{2,0,1:T(8,128)}, u32[]{:S(2)}, u32[]{:S(2)}) collective-permute-start(f32[256,1,512]{2,0,1:T(8,128)} %get-tuple-element.8), channel_id=1, source_target_pairs={{0,4},{4,8},{8,12},{12,16},{16,20},{20,24},{24,28},{28,0},{1,5},{5... | collective-permute-start | bytes 1572872 | tf_op jit(solution)/shard_map/ppermute | solution.py:16
  57.9 4.4 copy-start.5
  57.9 4.4 copy-start.6
  63.5 60.8 %collective-permute-start.7 = (f32[256,2,512]{0,2,1:T(8,128)S(1)}, f32[256,2,512]{0,2,1:T(8,128)}, u32[]{:S(2)}, u32[]{:S(2)}) collective-permute-start(f32[256,2,512]{0,2,1:T(8,128)S(1)} %get-tuple-element.16), channel_id=1, source_target_pairs={{0,4},{4,8},{8,12},{12,16},{16,20},{20,24},{24,28},{28,0},{1,5},{5... | collective-permute-start | bytes 3145736 | tf_op jit(solution)/shard_map/ppermute | solution.py:16
  73.9 50.5 %collective-permute-start.1 = (f32[256,1,512]{2,0,1:T(8,128)}, f32[256,1,512]{2,0,1:T(8,128)S(1)}, u32[]{:S(2)}, u32[]{:S(2)}) collective-permute-start(f32[256,1,512]{2,0,1:T(8,128)} %collective-permute-done), channel_id=1, source_target_pairs={{0,4},{4,8},{8,12},{12,16},{16,20},{20,24},{24,28},{28,0},{1,5},{5... | collective-permute-start | bytes 1572872 | tf_op jit(solution)/shard_map/ppermute | solution.py:16
  124.3 0.8 copy-start.7
  124.3 21.9 %collective-permute-start.2 = (f32[256,1,512]{2,0,1:T(8,128)S(1)}, f32[256,1,512]{2,0,1:T(8,128)}, u32[]{:S(2)}, u32[]{:S(2)}) collective-permute-start(f32[256,1,512]{2,0,1:T(8,128)S(1)} %collective-permute-done.1), channel_id=1, source_target_pairs={{0,4},{4,8},{8,12},{12,16},{16,20},{20,24},{24,28},{28,0},{1,5},{5... | collective-permute-start | bytes 1572872 | tf_op jit(solution)/shard_map/ppermute | solution.py:16
  125.2 60.4 %collective-permute-start.8 = (f32[256,2,512]{0,2,1:T(8,128)}, f32[256,2,512]{0,2,1:T(8,128)}, u32[]{:S(2)}, u32[]{:S(2)}) collective-permute-start(f32[256,2,512]{0,2,1:T(8,128)} %collective-permute-done.7), channel_id=1, source_target_pairs={{0,4},{4,8},{8,12},{12,16},{16,20},{20,24},{24,28},{28,0},{1,5},{5... | collective-permute-start | bytes 3145736 | tf_op jit(solution)/shard_map/ppermute | solution.py:16
  146.2 36.0 %collective-permute-start.3 = (f32[256,1,512]{2,0,1:T(8,128)}, f32[256,1,512]{2,0,1:T(8,128)}, u32[]{:S(2)}, u32[]{:S(2)}) collective-permute-start(f32[256,1,512]{2,0,1:T(8,128)} %collective-permute-done.2), channel_id=1, source_target_pairs={{0,4},{4,8},{8,12},{12,16},{16,20},{20,24},{24,28},{28,0},{1,5},{5... | collective-permute-start | bytes 1572872 | tf_op jit(solution)/shard_map/ppermute | solution.py:16
  152.8 6.2 %copy-start.2 = (f32[1,256,512]{1,2,0:T(8,128)S(1)}, f32[1,256,512]{1,2,0:T(8,128)}, u32[]{:S(2)}) copy-start(f32[1,256,512]{1,2,0:T(8,128)} %copy.32) | copy-start | bytes 1572868
  152.8 6.2 %copy-start.3 = (f32[1,256,512]{1,2,0:T(8,128)S(1)}, f32[1,256,512]{1,2,0:T(8,128)}, u32[]{:S(2)}) copy-start(f32[1,256,512]{1,2,0:T(8,128)} %copy.33) | copy-start | bytes 1572868
  152.8 6.2 %copy-start.4 = (f32[1,256,512]{1,2,0:T(8,128)S(1)}, f32[1,256,512]{1,2,0:T(8,128)}, u32[]{:S(2)}) copy-start(f32[1,256,512]{1,2,0:T(8,128)} %copy.34) | copy-start | bytes 1572868
  161.0 51.1 %collective-permute-start.14 = (f32[256,3,512]{0,2,1:T(8,128)}, f32[256,3,512]{0,2,1:T(8,128)}, u32[]{:S(2)}, u32[]{:S(2)}) collective-permute-start(f32[256,3,512]{0,2,1:T(8,128)} %get-tuple-element.14), channel_id=1, source_target_pairs={{0,4},{4,8},{8,12},{12,16},{16,20},{20,24},{24,28},{28,0},{1,5},{5... | collective-permute-start | bytes 4718600 | tf_op jit(solution)/shard_map/ppermute | solution.py:16
  182.2 22.5 %collective-permute-start.4 = (f32[256,1,512]{2,0,1:T(8,128)}, f32[256,1,512]{2,0,1:T(8,128)}, u32[]{:S(2)}, u32[]{:S(2)}) collective-permute-start(f32[256,1,512]{2,0,1:T(8,128)} %collective-permute-done.3), channel_id=1, source_target_pairs={{0,4},{4,8},{8,12},{12,16},{16,20},{20,24},{24,28},{28,0},{1,5},{5... | collective-permute-start | bytes 1572872 | tf_op jit(solution)/shard_map/ppermute | solution.py:16
  185.5 39.6 %collective-permute-start.9 = (f32[256,2,512]{0,2,1:T(8,128)}, f32[256,2,512]{0,2,1:T(8,128)}, u32[]{:S(2)}, u32[]{:S(2)}) collective-permute-start(f32[256,2,512]{0,2,1:T(8,128)} %collective-permute-done.8), channel_id=1, source_target_pairs={{0,4},{4,8},{8,12},{12,16},{16,20},{20,24},{24,28},{28,0},{1,5},{5... | collective-permute-start | bytes 3145736 | tf_op jit(solution)/shard_map/ppermute | solution.py:16
  204.6 16.7 %collective-permute-start.5 = (f32[256,1,512]{2,0,1:T(8,128)}, f32[256,1,512]{2,0,1:T(8,128)S(1)}, u32[]{:S(2)}, u32[]{:S(2)}) collective-permute-start(f32[256,1,512]{2,0,1:T(8,128)} %collective-permute-done.4), channel_id=1, source_target_pairs={{0,4},{4,8},{8,12},{12,16},{16,20},{20,24},{24,28},{28,0},{1,5},{5... | collective-permute-start | bytes 1572872 | tf_op jit(solution)/shard_map/ppermute | solution.py:16
  206.3 86.1 %reduce-scatter.7.cloned.1.call-start = ((), (), s32[]{:S(2)}) async-start(), calls=%async_computation.6 | async-start | bytes 1310720 | tf_op jit(solution)/shard_map/reduce_scatter | solution.py:58
  212.1 47.2 %collective-permute-start.15 = (f32[256,3,512]{0,2,1:T(8,128)}, f32[256,3,512]{0,2,1:T(8,128)S(1)}, u32[]{:S(2)}, u32[]{:S(2)}) collective-permute-start(f32[256,3,512]{0,2,1:T(8,128)} %collective-permute-done.14), channel_id=1, source_target_pairs={{0,4},{4,8},{8,12},{12,16},{16,20},{20,24},{24,28},{28,0},{1,5},{5... | collective-permute-start | bytes 4718600 | tf_op jit(solution)/shard_map/ppermute | solution.py:16
  221.4 22.5 %collective-permute-start.6 = (f32[256,1,512]{2,0,1:T(8,128)S(1)}, f32[256,1,512]{2,0,1:T(8,128)S(1)}, u32[]{:S(2)}, u32[]{:S(2)}) collective-permute-start(f32[256,1,512]{2,0,1:T(8,128)S(1)} %collective-permute-done.5), channel_id=1, source_target_pairs={{0,4},{4,8},{8,12},{12,16},{16,20},{20,24},{24,28},{28,0},{1,5},{5... | collective-permute-start | bytes 1572872 | tf_op jit(solution)/shard_map/ppermute | solution.py:16
  225.1 34.2 %collective-permute-start.10 = (f32[256,2,512]{0,2,1:T(8,128)}, f32[256,2,512]{0,2,1:T(8,128)}, u32[]{:S(2)}, u32[]{:S(2)}) collective-permute-start(f32[256,2,512]{0,2,1:T(8,128)} %collective-permute-done.9), channel_id=1, source_target_pairs={{0,4},{4,8},{8,12},{12,16},{16,20},{20,24},{24,28},{28,0},{1,5},{5... | collective-permute-start | bytes 3145736 | tf_op jit(solution)/shard_map/ppermute | solution.py:16
  251.6 40.8 %copy-start.1 = (f32[128,2048]{1,0:T(8,128)S(1)}, f32[128,2048]{1,0:T(8,128)}, u32[]{:S(2)}) copy-start(f32[128,2048]{1,0:T(8,128)} %reduce-scatter.5.cloned.1.call-done) | copy-start | bytes 3145732
  259.3 78.5 %all-gather.9.cloned.1.call-start = ((), (), s32[]{:S(2)}) async-start(), calls=%async_computation.7 | async-start | bytes 1310720 | tf_op jit(solution)/shard_map/all_gather | solution.py:65
  259.3 33.0 %collective-permute-start.16 = (f32[256,3,512]{0,2,1:T(8,128)S(1)}, f32[256,3,512]{0,2,1:T(8,128)}, u32[]{:S(2)}, u32[]{:S(2)}) collective-permute-start(f32[256,3,512]{0,2,1:T(8,128)S(1)} %collective-permute-done.15), channel_id=1, source_target_pairs={{0,4},{4,8},{8,12},{12,16},{16,20},{20,24},{24,28},{28,0},{1,5},{5... | collective-permute-start | bytes 4718600 | tf_op jit(solution)/shard_map/ppermute | solution.py:16
  259.4 33.0 %collective-permute-start.11 = (f32[256,2,512]{0,2,1:T(8,128)}, f32[256,2,512]{0,2,1:T(8,128)}, u32[]{:S(2)}, u32[]{:S(2)}) collective-permute-start(f32[256,2,512]{0,2,1:T(8,128)} %collective-permute-done.10), channel_id=1, source_target_pairs={{0,4},{4,8},{8,12},{12,16},{16,20},{20,24},{24,28},{28,0},{1,5},{5... | collective-permute-start | bytes 3145736 | tf_op jit(solution)/shard_map/ppermute | solution.py:16
  292.4 16.3 %collective-permute-start.12 = (f32[256,2,512]{0,2,1:T(8,128)}, f32[256,2,512]{0,2,1:T(8,128)}, u32[]{:S(2)}, u32[]{:S(2)}) collective-permute-start(f32[256,2,512]{0,2,1:T(8,128)} %collective-permute-done.11), channel_id=1, source_target_pairs={{0,4},{4,8},{8,12},{12,16},{16,20},{20,24},{24,28},{28,0},{1,5},{5... | collective-permute-start | bytes 3145736 | tf_op jit(solution)/shard_map/ppermute | solution.py:16
  292.4 33.2 %collective-permute-start.17 = (f32[256,3,512]{0,2,1:T(8,128)}, f32[256,3,512]{0,2,1:T(8,128)}, u32[]{:S(2)}, u32[]{:S(2)}) collective-permute-start(f32[256,3,512]{0,2,1:T(8,128)} %collective-permute-done.16), channel_id=1, source_target_pairs={{0,4},{4,8},{8,12},{12,16},{16,20},{20,24},{24,28},{28,0},{1,5},{5... | collective-permute-start | bytes 4718600 | tf_op jit(solution)/shard_map/ppermute | solution.py:16
  294.1 85.0 %reduce-scatter.9.cloned.1.call-start = ((), (), s32[]{:S(2)}) async-start(), calls=%async_computation.8 | async-start | bytes 1310720 | tf_op jit(solution)/shard_map/reduce_scatter | solution.py:58
  308.7 28.0 %collective-permute-start.13 = (f32[256,2,512]{0,2,1:T(8,128)}, f32[256,2,512]{0,2,1:T(8,128)S(1)}, u32[]{:S(2)}, u32[]{:S(2)}) collective-permute-start(f32[256,2,512]{0,2,1:T(8,128)} %collective-permute-done.12), channel_id=1, source_target_pairs={{0,4},{4,8},{8,12},{12,16},{16,20},{20,24},{24,28},{28,0},{1,5},{5... | collective-permute-start | bytes 3145736 | tf_op jit(solution)/shard_map/ppermute | solution.py:16
  325.5 28.1 %collective-permute-start.18 = (f32[256,3,512]{0,2,1:T(8,128)}, f32[256,3,512]{0,2,1:T(8,128)}, u32[]{:S(2)}, u32[]{:S(2)}) collective-permute-start(f32[256,3,512]{0,2,1:T(8,128)} %collective-permute-done.17), channel_id=1, source_target_pairs={{0,4},{4,8},{8,12},{12,16},{16,20},{20,24},{24,28},{28,0},{1,5},{5... | collective-permute-start | bytes 4718600 | tf_op jit(solution)/shard_map/ppermute | solution.py:16
  352.8 55.1 %all-gather.11.cloned.1.call-start = ((), (), s32[]{:S(2)}) async-start(), calls=%async_computation.9 | async-start | bytes 1310720 | tf_op jit(solution)/shard_map/all_gather | solution.py:65
  353.6 22.0 %collective-permute-start.19 = (f32[256,3,512]{0,2,1:T(8,128)}, f32[256,3,512]{0,2,1:T(8,128)}, u32[]{:S(2)}, u32[]{:S(2)}) collective-permute-start(f32[256,3,512]{0,2,1:T(8,128)} %collective-permute-done.18), channel_id=1, source_target_pairs={{0,4},{4,8},{8,12},{12,16},{16,20},{20,24},{24,28},{28,0},{1,5},{5... | collective-permute-start | bytes 4718600 | tf_op jit(solution)/shard_map/ppermute | solution.py:16
  375.6 22.0 %collective-permute-start.20 = (f32[256,3,512]{0,2,1:T(8,128)}, f32[256,3,512]{0,2,1:T(8,128)}, u32[]{:S(2)}, u32[]{:S(2)}) collective-permute-start(f32[256,3,512]{0,2,1:T(8,128)} %collective-permute-done.19), channel_id=1, source_target_pairs={{0,4},{4,8},{8,12},{12,16},{16,20},{20,24},{24,28},{28,0},{1,5},{5... | collective-permute-start | bytes 4718600 | tf_op jit(solution)/shard_map/ppermute | solution.py:16
  380.8 72.7 %reduce-scatter.11.cloned.1.call-start = ((), (), s32[]{:S(2)}) async-start(), calls=%async_computation.10 | async-start | bytes 1310720 | tf_op jit(solution)/shard_map/reduce_scatter | solution.py:58
  425.4 57.0 %all-gather.13.cloned.1.call-start = ((), (), s32[]{:S(2)}) async-start(), calls=%async_computation.11 | async-start | bytes 1310720 | tf_op jit(solution)/shard_map/all_gather | solution.py:65
Sparse Core Ops, SparseCore 0:
  50.0 125.9 reduce-scatter.4
  206.5 27.7 all-gather.6
  259.4 26.1 reduce-scatter.6
  294.2 28.0 all-gather.8
  352.9 26.1 reduce-scatter.8
  381.4 26.4 all-gather.10
  425.5 27.9 reduce-scatter.10
  455.9 26.4 all-gather.12
